TPU v7x, 32 devices: a whole 2x2x4 slice. The times are simulated.
32 devices in a mesh: lon: 8 (over z, core), lat: 4 (over y, x).
Axes of the slice: x: 2, y: 2, z: 4, core: 2. Of those that a mesh axis runs over, the one named last changes fastest.
Arguments:
- adjoint_state: float32 [4, 20, 256, 1024], P(None, None, 'lat', 'lon'), may hold values from -6 to 6
- coefficients: float32 [2, 256, 1024], P(None, 'lat', 'lon'), may hold values from 0.02 to 0.22
- mask: int32 [20, 256, 1024], P(None, 'lat', 'lon'), may hold values from 0 to 1, as said below
- bottom: int32 [256, 1024], P('lat', 'lon'), may hold values from 0 to 20, as said below
Outputs:
- sensitivity: float32 [4, 20, 256, 1024], P(None, None, 'lat', 'lon')
Inputs may be any that keep to these rules, and one draw needn't show every extreme that they name: `mask`: 1 marks an ocean cell; a cell is 1 only at levels below its column's entry of bottom. `bottom`: levels reached by the column, 0 for land columns.
All inputs are finite; a program needn't handle non-finite values.
Results may differ from a plain program's by a relative error of at most 0.00002.
Values sent between devices are 32-bit elements; how exact they have to be, the bound alone decides.
A program may use at most 128 MiB of HBM per device.

v0:
```python
import functools

import jax
import jax.numpy as jnp
from jax import lax
from jax.experimental import pallas as pl
from jax.experimental.pallas import tpu as pltpu
from jax.sharding import PartitionSpec as P

ITERS = 4
GROUPS = 2
CHUNK = 16
PAD = 8

HALINE_CONTRACTION = 0.8
PRESSURE_SCALE = 0.05
BOTTOM_DRAG = 0.3
CORIOLIS_SCALE = 0.3

KEEP, WEST, EAST, SOUTH, NORTH = range(5)


def kernel(
    n_lon, n_lat, levels, rows, cols, groups,
    state, coef, mask, bottom, out,
    buf, wet, mraw, bot, cf, stat, cor, top, rho, side, upper,
    csend, from_west, from_east, to_north, to_south, from_south, from_north,
    in_sem, out_sem, send_sem, recv_sem,
):
    per = levels // groups
    chunk = CHUNK
    lon, lat = lax.axis_index("lon"), lax.axis_index("lat")
    west, east = lax.rem(lon + n_lon - 1, n_lon), lax.rem(lon + 1, n_lon)
    is_top = lat == n_lat - 1
    not_top = lat < n_lat - 1
    not_low = lat > 0
    mirror = n_lon - 1 - lon

    def base(g):
        return levels - (g + 1) * per

    small = [
        pltpu.make_async_copy(coef, cf, in_sem.at[groups, 0]),
        pltpu.make_async_copy(bottom, bot, in_sem.at[groups, 1]),
    ]
    loads = [
        [
            pltpu.make_async_copy(
                state.at[:, pl.ds(base(g), per)],
                buf.at[0, :, pl.ds(base(g), per), pl.ds(PAD, rows), :],
                in_sem.at[g, 0],
            ),
            pltpu.make_async_copy(
                mask.at[pl.ds(base(g), per)], mraw.at[pl.ds(base(g), per)], in_sem.at[g, 1]
            ),
        ]
        for g in range(groups)
    ]
    for copy in small:
        copy.start()
    for pair in loads:
        for copy in pair:
            copy.start()

    barrier = pltpu.get_barrier_semaphore()

    def greet(target):
        pl.semaphore_signal(barrier, inc=1, device_id=target, device_id_type=pl.DeviceIdType.MESH)

    greet({"lon": west, "lat": lat})
    greet({"lon": east, "lat": lat})

    @pl.when(is_top)
    def _():
        greet({"lon": mirror, "lat": lat})

    @pl.when(not_top)
    def _():
        greet({"lon": lon, "lat": lat + 1})

    @pl.when(not_low)
    def _():
        greet({"lon": lon, "lat": lat - 1})

    pl.semaphore_wait(barrier, 3 + jnp.minimum(lat, 1))

    def remote(source, target, stage, g, sent, received, where):
        return pltpu.make_async_remote_copy(
            src_ref=source.at[stage, g],
            dst_ref=target.at[stage, g],
            send_sem=send_sem.at[stage, g, sent],
            recv_sem=recv_sem.at[stage, g, received],
            device_id=where,
            device_id_type=pl.DeviceIdType.MESH,
        )

    def go_west(stage, g):
        return remote(csend, from_east, stage, g, 0, 0, {"lon": west, "lat": lat})

    def go_east(stage, g):
        return remote(csend, from_west, stage, g, 1, 1, {"lon": east, "lat": lat})

    def go_north(stage, g):
        return remote(to_north, from_south, stage, g, 2, 2, {"lon": lon, "lat": lat + 1})

    def go_fold(stage, g):
        return remote(to_north, from_north, stage, g, 2, 3, {"lon": mirror, "lat": lat})

    def go_south(stage, g):
        return remote(to_south, from_north, stage, g, 3, 3, {"lon": lon, "lat": lat - 1})

    def send(stage, g):
        go_west(stage, g).start()
        go_east(stage, g).start()

        @pl.when(is_top)
        def _():
            go_fold(stage, g).start()

        @pl.when(not_top)
        def _():
            go_north(stage, g).start()

        @pl.when(not_low)
        def _():
            go_south(stage, g).start()

    def sent(stage, g):
        go_west(stage, g).wait_send()
        go_east(stage, g).wait_send()

        @pl.when(is_top)
        def _():
            go_fold(stage, g).wait_send()

        @pl.when(not_top)
        def _():
            go_north(stage, g).wait_send()

        @pl.when(not_low)
        def _():
            go_south(stage, g).wait_send()

    lane_c = lax.broadcasted_iota(jnp.int32, (chunk, cols), 1)
    half_c = lane_c >> 1
    first_lane, last_lane = lane_c == 0, lane_c == cols - 1

    def put(stage, g, j, r0, values):
        span = pl.ds(r0, chunk)
        packed = csend[stage, g, span, :]
        for f in range(4):
            fl = f * per + j
            packed = jnp.where(half_c == fl, pltpu.roll(values[f], 2 * fl + 1, 1), packed)
        csend[stage, g, span, :] = packed
        for f in range(4):
            fl = f * per + j
            if r0 == 0:
                to_south[stage, g, pl.ds(fl, 1), :] = values[f][0:1]
            if r0 + chunk == rows:
                to_north[stage, g, pl.ds(fl, 1), :] = values[f][chunk - 1 : chunk]

    csend[...] = jnp.zeros_like(csend)
    to_north[...] = jnp.zeros_like(to_north)
    to_south[...] = jnp.zeros_like(to_south)

    @pl.when(lat == 0)
    def _():
        from_south[...] = jnp.zeros_like(from_south)

    for copy in small:
        copy.wait()

    def settle(stage, g):
        go_west(stage, g).wait_recv()
        go_east(stage, g).wait_recv()
        go_fold(stage, g).wait_recv()

        @pl.when(not_low)
        def _():
            landed = remote(to_north, from_south, stage, g, 2, 2, {"lon": mirror, "lat": lat})
            landed.wait_recv()

        lane = lax.broadcasted_iota(jnp.int32, (rows, cols), 1)
        side[...] = jnp.where(
            (lane & 1) == 0, from_west[stage, g], pltpu.roll(from_east[stage, g], cols - 2, 1)
        )

        @pl.when(not_top)
        def _():
            upper[...] = from_north[stage, g]

        @pl.when(is_top)
        def _():
            line = from_north[stage, g]
            place = lax.broadcasted_iota(jnp.int32, line.shape, 1)
            item = lax.broadcasted_iota(jnp.int32, line.shape, 0)
            bit = 1
            while bit < cols:
                line = jnp.where(
                    (place & bit) == 0, pltpu.roll(line, cols - bit, 1), pltpu.roll(line, bit, 1)
                )
                bit *= 2
            flip = (item >= 2 * per) & (item < 4 * per)
            upper[...] = jnp.where(flip, -line, line)

    for g in range(groups):
        for copy in loads[g]:
            copy.wait()

        def first(i, carry, g=g):
            j = per - 1 - i
            level = base(g) + j
            for r0 in range(0, rows, chunk):
                w = mraw[level, pl.ds(r0, chunk), :].astype(jnp.float32)
                wet[level, pl.ds(r0, chunk), :] = w
                values = []
                for f in range(4):
                    t = w * buf[0, f, level, pl.ds(PAD + r0, chunk), :]
                    buf[0, f, level, pl.ds(PAD + r0, chunk), :] = t
                    values.append(t)
                put(0, g, j, r0, values)
            return carry

        lax.fori_loop(0, per, first, 0)
        if g == 0:
            for n in range(2):
                fl = 4 * per + n
                for r0 in range(0, rows, chunk):
                    packed = csend[0, 0, pl.ds(r0, chunk), :]
                    value = cf[n, pl.ds(r0, chunk), :]
                    csend[0, 0, pl.ds(r0, chunk), :] = jnp.where(
                        half_c == fl, pltpu.roll(value, 2 * fl + 1, 1), packed
                    )
                to_south[0, 0, fl : fl + 1, :] = cf[n, 0:1, :]
                to_north[0, 0, fl : fl + 1, :] = cf[n, rows - 1 : rows, :]
        send(0, g)

    row = lax.broadcasted_iota(jnp.int32, (rows, cols), 0)
    lane = lax.broadcasted_iota(jnp.int32, (rows, cols), 1)
    cor[...] = CORIOLIS_SCALE * (
        2.0 * ((lat * rows + row).astype(jnp.float32) + 0.5) / (n_lat * rows) - 1.0
    )
    top_device = jnp.where(is_top, 1.0, 0.0)
    top[...] = jnp.where(row == rows - 1, top_device, 0.0)
    bot[...] = bot[...] - 1

    for step in range(ITERS):
        cur, nxt = step % 2, (step + 1) % 2
        last = step == ITERS - 1
        rho[...] = jnp.zeros_like(rho)
        for g in range(groups):
            settle(step, g)
            if step == 0 and g == 0:
                for n in range(2):
                    fl = 4 * per + n
                    value = cf[n]
                    ends = pltpu.roll(side[...], cols - 2 * fl, 1)
                    stat[n, KEEP] = 1.0 - 4.0 * value
                    stat[n, WEST] = jnp.where(lane == 0, ends, pltpu.roll(value, 1, 1))
                    stat[n, EAST] = jnp.where(lane == cols - 1, ends, pltpu.roll(value, cols - 1, 1))
                    stat[n, SOUTH] = jnp.where(
                        row == 0, from_south[0, 0, fl : fl + 1, :], pltpu.roll(value, 1, 0)
                    )
                    stat[n, NORTH] = jnp.where(
                        row == rows - 1, upper[fl : fl + 1, :], pltpu.roll(value, rows - 1, 0)
                    )

            def advance(i, carry, g=g, step=step, cur=cur, nxt=nxt, last=last):
                j = per - 1 - i
                level = base(g) + j
                for f in range(4):
                    fl = f * per + j
                    buf[cur, f, level, PAD - 1 : PAD, :] = from_south[step, g, pl.ds(fl, 1), :]
                    buf[cur, f, level, PAD + rows : PAD + rows + 1, :] = upper[pl.ds(fl, 1), :]
                for r0 in range(0, rows, chunk):
                    span = pl.ds(r0, chunk)
                    edges = side[span, :]
                    here, near, wests, souths, norths = [], [], [], [], []
                    for f in range(4):
                        n = f // 2
                        fl = f * per + j
                        t = buf[cur, f, level, PAD + r0 : PAD + r0 + chunk, :]
                        ends = pltpu.roll(edges, lax.rem(cols - 2 * fl, cols), 1)
                        t_west = jnp.where(first_lane, ends, pltpu.roll(t, 1, 1))
                        t_east = jnp.where(last_lane, ends, pltpu.roll(t, cols - 1, 1))
                        t_south = buf[cur, f, level, PAD + r0 - 1 : PAD + r0 - 1 + chunk, :]
                        t_north = buf[cur, f, level, PAD + r0 + 1 : PAD + r0 + 1 + chunk, :]
                        near.append(
                            stat[n, WEST, span, :] * t_west
                            + stat[n, EAST, span, :] * t_east
                            + stat[n, SOUTH, span, :] * t_south
                            + stat[n, NORTH, span, :] * t_north
                        )
                        here.append(t)
                        wests.append(t_west)
                        souths.append(t_south)
                        norths.append(t_north)
                    q = here[2] + here[3] - wests[2] - souths[3]
                    if r0 + chunk == rows:
                        q = q + top[span, :] * norths[3]
                    run = rho[span, :] + PRESSURE_SCALE * q
                    rho[span, :] = run
                    w = wet[level, span, :]
                    keep = stat[0, KEEP, span, :]
                    drag = jnp.where(bot[span, :] == level, BOTTOM_DRAG, 0.0)
                    keep_uv = stat[1, KEEP, span, :] - drag
                    c = cor[span, :]
                    values = [
                        w * (keep * here[0] + near[0] + run),
                        w * (keep * here[1] + near[1] - HALINE_CONTRACTION * run),
                        w * (keep_uv * here[2] + near[2] - c * here[3]),
                        w * (keep_uv * here[3] + near[3] + c * here[2]),
                    ]
                    for f in range(4):
                        buf[nxt, f, level, PAD + r0 : PAD + r0 + chunk, :] = values[f]
                    if not last:
                        put(step + 1, g, j, r0, values)
                return carry

            lax.fori_loop(0, per, advance, 0)
            if not last:
                send(step + 1, g)
            else:
                store(out, buf, out_sem, nxt, base(g), per, rows, g).start()

    for stage in range(ITERS):
        for g in range(groups):
            sent(stage, g)
    for g in range(groups):
        store(out, buf, out_sem, ITERS % 2, base(g), per, rows, g).wait()


def store(out, buf, out_sem, slot, base, per, rows, g):
    return pltpu.make_async_copy(
        buf.at[slot, :, pl.ds(base, per), pl.ds(PAD, rows), :],
        out.at[:, pl.ds(base, per)],
        out_sem.at[g],
    )


def solution(mesh):
    n_lon, n_lat = mesh.shape["lon"], mesh.shape["lat"]
    placed = (
        P(None, None, "lat", "lon"),
        P(None, "lat", "lon"),
        P(None, "lat", "lon"),
        P("lat", "lon"),
    )

    def local(adjoint_state, coefficients, mask, bottom):
        levels, rows, cols = mask.shape
        groups = GROUPS
        per = levels // groups
        lines = -(-(4 * per + 2) // 8) * 8
        f32 = jnp.float32
        dma = pltpu.SemaphoreType.DMA
        return pl.pallas_call(
            functools.partial(kernel, n_lon, n_lat, levels, rows, cols, groups),
            out_shape=jax.ShapeDtypeStruct(adjoint_state.shape, f32),
            in_specs=[pl.BlockSpec(memory_space=pl.ANY)] * 4,
            out_specs=pl.BlockSpec(memory_space=pl.ANY),
            scratch_shapes=[
                pltpu.VMEM((2, 4, levels, rows + 2 * PAD, cols), f32),
                pltpu.VMEM((levels, rows, cols), f32),
                pltpu.VMEM((levels, rows, cols), jnp.int32),
                pltpu.VMEM((rows, cols), jnp.int32),
                pltpu.VMEM((2, rows, cols), f32),
                pltpu.VMEM((2, 5, rows, cols), f32),
                pltpu.VMEM((rows, cols), f32),
                pltpu.VMEM((rows, cols), f32),
                pltpu.VMEM((rows, cols), f32),
                pltpu.VMEM((rows, cols), f32),
                pltpu.VMEM((lines, cols), f32),
                pltpu.VMEM((ITERS, groups, rows, cols), f32),
                pltpu.VMEM((ITERS, groups, rows, cols), f32),
                pltpu.VMEM((ITERS, groups, rows, cols), f32),
                pltpu.VMEM((ITERS, groups, lines, cols), f32),
                pltpu.VMEM((ITERS, groups, lines, cols), f32),
                pltpu.VMEM((ITERS, groups, lines, cols), f32),
                pltpu.VMEM((ITERS, groups, lines, cols), f32),
                dma((groups + 1, 2)),
                dma((groups,)),
                dma((ITERS, groups, 4)),
                dma((ITERS, groups, 4)),
            ],
            compiler_params=pltpu.CompilerParams(
                collective_id=0, has_side_effects=True, vmem_limit_bytes=40 << 20
            ),
            name="adjoint_steps",
        )(adjoint_state, coefficients, mask, bottom)

    return jax.shard_map(
        local, mesh=mesh, in_specs=placed, out_specs=P(None, None, "lat", "lon"), check_vma=False
    )
```

profile of v0, /device:TPU:7, one launch (start us, length us, event | category | flops | bytes accessed | tf_op | source)
XLA Modules:
  0.0 43.8 jit_solution(7177921359653020996)
XLA Ops:
  0.0 0.0 copy-start
  0.0 1.7 %copy-done = f32[4,20,64,128]{3,2,1,0:T(8,128)S(1)} copy-done((f32[4,20,64,128]{3,2,1,0:T(8,128)S(1)}, f32[4,20,64,128]{3,2,1,0:T(8,128)}, u32[]{:S(2)}) %copy-start) | copy-done | bytes 2621464
  1.7 0.0 copy-start.1
  1.7 1.1 %copy-done.1 = s32[20,64,128]{2,1,0:T(8,128)S(1)} copy-done((s32[20,64,128]{2,1,0:T(8,128)S(1)}, s32[20,64,128]{2,1,0:T(8,128)}, u32[]{:S(2)}) %copy-start.1) | copy-done | bytes 655384
  2.8 0.0 copy-start.2
  2.8 0.8 %copy-done.2 = f32[2,64,128]{2,1,0:T(8,128)S(1)} copy-done((f32[2,64,128]{2,1,0:T(8,128)S(1)}, f32[2,64,128]{2,1,0:T(8,128)}, u32[]{:S(2)}) %copy-start.2) | copy-done | bytes 65560
  3.7 0.0 copy-start.3
  3.7 0.8 %copy-done.3 = s32[64,128]{1,0:T(8,128)S(1)} copy-done((s32[64,128]{1,0:T(8,128)S(1)}, s32[64,128]{1,0:T(8,128)}, u32[]{:S(2)}) %copy-start.3) | copy-done | bytes 32792
  4.4 37.9 %adjoint_steps.1 = f32[4,20,64,128]{3,2,1,0:T(8,128)S(1)} custom-call(f32[4,20,64,128]{3,2,1,0:T(8,128)S(1)} %copy-done, f32[2,64,128]{2,1,0:T(8,128)S(1)} %copy-done.2, s32[20,64,128]{2,1,0:T(8,128)S(1)} %copy-done.1, s32[64,128]{1,0:T(8,128)S(1)} %copy-done.3), custom_call_target="tpu_custom_call" | custom-call | tf_op jit(solution)/shard_map/adjoint_steps/pallas_call | solution.py:357
  42.3 1.5 %copy.6 = f32[4,20,64,128]{3,2,1,0:T(8,128)} copy(f32[4,20,64,128]{3,2,1,0:T(8,128)S(1)} %adjoint_steps.1) | data formatting | bytes 5242880
Async XLA Ops:
  0.0 1.7 %copy-start = (f32[4,20,64,128]{3,2,1,0:T(8,128)S(1)}, f32[4,20,64,128]{3,2,1,0:T(8,128)}, u32[]{:S(2)}) copy-start(f32[4,20,64,128]{3,2,1,0:T(8,128)} %state.1) | copy-start | bytes 7864324
  1.7 1.1 %copy-start.1 = (s32[20,64,128]{2,1,0:T(8,128)S(1)}, s32[20,64,128]{2,1,0:T(8,128)}, u32[]{:S(2)}) copy-start(s32[20,64,128]{2,1,0:T(8,128)} %mask.1) | copy-start | bytes 1966084
  2.8 0.8 %copy-start.2 = (f32[2,64,128]{2,1,0:T(8,128)S(1)}, f32[2,64,128]{2,1,0:T(8,128)}, u32[]{:S(2)}) copy-start(f32[2,64,128]{2,1,0:T(8,128)} %coef.1) | copy-start | bytes 196612
  3.7 0.8 %copy-start.3 = (s32[64,128]{1,0:T(8,128)S(1)}, s32[64,128]{1,0:T(8,128)}, u32[]{:S(2)}) copy-start(s32[64,128]{1,0:T(8,128)} %bottom.1) | copy-start | bytes 98308
where the time goes:
time: 44.1 us; the launch traced here: 43.8 us
  Pallas kernels  37.9 us (86%)
  local copies, waits for them, and re-layouts  5.92 us (13%)
    pallas_call x1, Pallas kernels, local(): pl.pallas_call(functools.partial(kernel, n_lon, n_lat, levels, rows, cols...  37.9 us
    unnamed x9, local copies, waits for them, and re-layouts  5.92 us

commit v1 on v0

--- a/solution.py
+++ b/solution.py
@@ -8,7 +8,7 @@
 from jax.sharding import PartitionSpec as P
 
 ITERS = 4
-GROUPS = 2
+GROUPS = 4
 CHUNK = 16
 PAD = 8
 
@@ -23,12 +23,13 @@
 def kernel(
     n_lon, n_lat, levels, rows, cols, groups,
     state, coef, mask, bottom, out,
-    buf, wet, mraw, bot, cf, stat, cor, top, rho, side, upper,
+    buf_a, buf_b, wet, mraw, bot, cf, stat, cor, top, rho, side, upper,
     csend, from_west, from_east, to_north, to_south, from_south, from_north,
     in_sem, out_sem, send_sem, recv_sem,
 ):
     per = levels // groups
     chunk = CHUNK
+    bufs = (buf_a, buf_b)
     lon, lat = lax.axis_index("lon"), lax.axis_index("lat")
     west, east = lax.rem(lon + n_lon - 1, n_lon), lax.rem(lon + 1, n_lon)
     is_top = lat == n_lat - 1
@@ -43,23 +44,23 @@
         pltpu.make_async_copy(coef, cf, in_sem.at[groups, 0]),
         pltpu.make_async_copy(bottom, bot, in_sem.at[groups, 1]),
     ]
-    loads = [
-        [
+
+    def load(g):
+        return [
             pltpu.make_async_copy(
                 state.at[:, pl.ds(base(g), per)],
-                buf.at[0, :, pl.ds(base(g), per), pl.ds(PAD, rows), :],
+                bufs[0].at[:, pl.ds(base(g), per), pl.ds(PAD, rows), :],
                 in_sem.at[g, 0],
             ),
             pltpu.make_async_copy(
                 mask.at[pl.ds(base(g), per)], mraw.at[pl.ds(base(g), per)], in_sem.at[g, 1]
             ),
         ]
-        for g in range(groups)
-    ]
+
     for copy in small:
         copy.start()
-    for pair in loads:
-        for copy in pair:
+    for g in range(groups):
+        for copy in load(g):
             copy.start()
 
     barrier = pltpu.get_barrier_semaphore()
@@ -192,22 +193,17 @@
         @pl.when(is_top)
         def _():
             line = from_north[stage, g]
-            place = lax.broadcasted_iota(jnp.int32, line.shape, 1)
             item = lax.broadcasted_iota(jnp.int32, line.shape, 0)
-            bit = 1
-            while bit < cols:
-                line = jnp.where(
-                    (place & bit) == 0, pltpu.roll(line, cols - bit, 1), pltpu.roll(line, bit, 1)
-                )
-                bit *= 2
+            place = cols - 1 - lax.broadcasted_iota(jnp.int32, line.shape, 1)
+            line = jnp.take_along_axis(line, place, axis=1, mode="promise_in_bounds")
             flip = (item >= 2 * per) & (item < 4 * per)
             upper[...] = jnp.where(flip, -line, line)
 
-    for g in range(groups):
-        for copy in loads[g]:
+    def begin(g, carry):
+        for copy in load(g):
             copy.wait()
 
-        def first(i, carry, g=g):
+        def first(i, carry):
             j = per - 1 - i
             level = base(g) + j
             for r0 in range(0, rows, chunk):
@@ -215,14 +211,16 @@
                 wet[level, pl.ds(r0, chunk), :] = w
                 values = []
                 for f in range(4):
-                    t = w * buf[0, f, level, pl.ds(PAD + r0, chunk), :]
-                    buf[0, f, level, pl.ds(PAD + r0, chunk), :] = t
+                    t = w * bufs[0][f, level, pl.ds(PAD + r0, chunk), :]
+                    bufs[0][f, level, pl.ds(PAD + r0, chunk), :] = t
                     values.append(t)
                 put(0, g, j, r0, values)
             return carry
 
         lax.fori_loop(0, per, first, 0)
-        if g == 0:
+
+        @pl.when(g == 0)
+        def _():
             for n in range(2):
                 fl = 4 * per + n
                 for r0 in range(0, rows, chunk):
@@ -233,7 +231,11 @@
                     )
                 to_south[0, 0, fl : fl + 1, :] = cf[n, 0:1, :]
                 to_north[0, 0, fl : fl + 1, :] = cf[n, rows - 1 : rows, :]
+
         send(0, g)
+        return carry
+
+    lax.fori_loop(0, groups, begin, 0)
 
     row = lax.broadcasted_iota(jnp.int32, (rows, cols), 0)
     lane = lax.broadcasted_iota(jnp.int32, (rows, cols), 1)
@@ -244,95 +246,110 @@
     top[...] = jnp.where(row == rows - 1, top_device, 0.0)
     bot[...] = bot[...] - 1
 
+    def weigh():
+        for n in range(2):
+            fl = 4 * per + n
+            value = cf[n]
+            ends = pltpu.roll(side[...], cols - 2 * fl, 1)
+            stat[n, KEEP] = 1.0 - 4.0 * value
+            stat[n, WEST] = jnp.where(lane == 0, ends, pltpu.roll(value, 1, 1))
+            stat[n, EAST] = jnp.where(lane == cols - 1, ends, pltpu.roll(value, cols - 1, 1))
+            stat[n, SOUTH] = jnp.where(
+                row == 0, from_south[0, 0, fl : fl + 1, :], pltpu.roll(value, 1, 0)
+            )
+            stat[n, NORTH] = jnp.where(
+                row == rows - 1, upper[fl : fl + 1, :], pltpu.roll(value, rows - 1, 0)
+            )
+
+    def turn(step, g, carry):
+        cur, nxt = bufs[step % 2], bufs[(step + 1) % 2]
+        last = step == ITERS - 1
+        settle(step, g)
+
+        if step == 0:
+
+            @pl.when(g == 0)
+            def _():
+                weigh()
+
+        @pl.when(g == 0)
+        def _():
+            rho[...] = jnp.zeros_like(rho)
+
+        def advance(i, carry):
+            j = per - 1 - i
+            level = base(g) + j
+            for f in range(4):
+                fl = f * per + j
+                cur[f, level, PAD - 1 : PAD, :] = from_south[step, g, pl.ds(fl, 1), :]
+                cur[f, level, PAD + rows : PAD + rows + 1, :] = upper[pl.ds(fl, 1), :]
+            for r0 in range(0, rows, chunk):
+                span = pl.ds(r0, chunk)
+                edges = side[span, :]
+                here, near, wests, souths, norths = [], [], [], [], []
+                for f in range(4):
+                    n = f // 2
+                    fl = f * per + j
+                    t = cur[f, level, PAD + r0 : PAD + r0 + chunk, :]
+                    ends = pltpu.roll(edges, lax.rem(cols - 2 * fl, cols), 1)
+                    t_west = jnp.where(first_lane, ends, pltpu.roll(t, 1, 1))
+                    t_east = jnp.where(last_lane, ends, pltpu.roll(t, cols - 1, 1))
+                    t_south = cur[f, level, PAD + r0 - 1 : PAD + r0 - 1 + chunk, :]
+                    t_north = cur[f, level, PAD + r0 + 1 : PAD + r0 + 1 + chunk, :]
+                    near.append(
+                        stat[n, WEST, span, :] * t_west
+                        + stat[n, EAST, span, :] * t_east
+                        + stat[n, SOUTH, span, :] * t_south
+                        + stat[n, NORTH, span, :] * t_north
+                    )
+                    here.append(t)
+                    wests.append(t_west)
+                    souths.append(t_south)
+                    norths.append(t_north)
+                q = here[2] + here[3] - wests[2] - souths[3]
+                if r0 + chunk == rows:
+                    q = q + top[span, :] * norths[3]
+                run = rho[span, :] + PRESSURE_SCALE * q
+                rho[span, :] = run
+                w = wet[level, span, :]
+                keep = stat[0, KEEP, span, :]
+                drag = jnp.where(bot[span, :] == level, BOTTOM_DRAG, 0.0)
+                keep_uv = stat[1, KEEP, span, :] - drag
+                c = cor[span, :]
+                values = [
+                    w * (keep * here[0] + near[0] + run),
+                    w * (keep * here[1] + near[1] - HALINE_CONTRACTION * run),
+                    w * (keep_uv * here[2] + near[2] - c * here[3]),
+                    w * (keep_uv * here[3] + near[3] + c * here[2]),
+                ]
+                for f in range(4):
+                    nxt[f, level, PAD + r0 : PAD + r0 + chunk, :] = values[f]
+                if not last:
+                    put(step + 1, g, j, r0, values)
+            return carry
+
+        lax.fori_loop(0, per, advance, 0)
+        if not last:
+            send(step + 1, g)
+        else:
+            store(out, nxt, out_sem, base(g), per, rows, g).start()
+        return carry
+
     for step in range(ITERS):
-        cur, nxt = step % 2, (step + 1) % 2
-        last = step == ITERS - 1
-        rho[...] = jnp.zeros_like(rho)
-        for g in range(groups):
-            settle(step, g)
-            if step == 0 and g == 0:
-                for n in range(2):
-                    fl = 4 * per + n
-                    value = cf[n]
-                    ends = pltpu.roll(side[...], cols - 2 * fl, 1)
-                    stat[n, KEEP] = 1.0 - 4.0 * value
-                    stat[n, WEST] = jnp.where(lane == 0, ends, pltpu.roll(value, 1, 1))
-                    stat[n, EAST] = jnp.where(lane == cols - 1, ends, pltpu.roll(value, cols - 1, 1))
-                    stat[n, SOUTH] = jnp.where(
-                        row == 0, from_south[0, 0, fl : fl + 1, :], pltpu.roll(value, 1, 0)
-                    )
-                    stat[n, NORTH] = jnp.where(
-                        row == rows - 1, upper[fl : fl + 1, :], pltpu.roll(value, rows - 1, 0)
-                    )
-
-            def advance(i, carry, g=g, step=step, cur=cur, nxt=nxt, last=last):
-                j = per - 1 - i
-                level = base(g) + j
-                for f in range(4):
-                    fl = f * per + j
-                    buf[cur, f, level, PAD - 1 : PAD, :] = from_south[step, g, pl.ds(fl, 1), :]
-                    buf[cur, f, level, PAD + rows : PAD + rows + 1, :] = upper[pl.ds(fl, 1), :]
-                for r0 in range(0, rows, chunk):
-                    span = pl.ds(r0, chunk)
-                    edges = side[span, :]
-                    here, near, wests, souths, norths = [], [], [], [], []
-                    for f in range(4):
-                        n = f // 2
-                        fl = f * per + j
-                        t = buf[cur, f, level, PAD + r0 : PAD + r0 + chunk, :]
-                        ends = pltpu.roll(edges, lax.rem(cols - 2 * fl, cols), 1)
-                        t_west = jnp.where(first_lane, ends, pltpu.roll(t, 1, 1))
-                        t_east = jnp.where(last_lane, ends, pltpu.roll(t, cols - 1, 1))
-                        t_south = buf[cur, f, level, PAD + r0 - 1 : PAD + r0 - 1 + chunk, :]
-                        t_north = buf[cur, f, level, PAD + r0 + 1 : PAD + r0 + 1 + chunk, :]
-                        near.append(
-                            stat[n, WEST, span, :] * t_west
-                            + stat[n, EAST, span, :] * t_east
-                            + stat[n, SOUTH, span, :] * t_south
-                            + stat[n, NORTH, span, :] * t_north
-                        )
-                        here.append(t)
-                        wests.append(t_west)
-                        souths.append(t_south)
-                        norths.append(t_north)
-                    q = here[2] + here[3] - wests[2] - souths[3]
-                    if r0 + chunk == rows:
-                        q = q + top[span, :] * norths[3]
-                    run = rho[span, :] + PRESSURE_SCALE * q
-                    rho[span, :] = run
-                    w = wet[level, span, :]
-                    keep = stat[0, KEEP, span, :]
-                    drag = jnp.where(bot[span, :] == level, BOTTOM_DRAG, 0.0)
-                    keep_uv = stat[1, KEEP, span, :] - drag
-                    c = cor[span, :]
-                    values = [
-                        w * (keep * here[0] + near[0] + run),
-                        w * (keep * here[1] + near[1] - HALINE_CONTRACTION * run),
-                        w * (keep_uv * here[2] + near[2] - c * here[3]),
-                        w * (keep_uv * here[3] + near[3] + c * here[2]),
-                    ]
-                    for f in range(4):
-                        buf[nxt, f, level, PAD + r0 : PAD + r0 + chunk, :] = values[f]
-                    if not last:
-                        put(step + 1, g, j, r0, values)
-                return carry
-
-            lax.fori_loop(0, per, advance, 0)
-            if not last:
-                send(step + 1, g)
-            else:
-                store(out, buf, out_sem, nxt, base(g), per, rows, g).start()
-
-    for stage in range(ITERS):
-        for g in range(groups):
-            sent(stage, g)
+        lax.fori_loop(0, groups, functools.partial(turn, step), 0)
+
+    def drain(m, carry):
+        sent(m // groups, m % groups)
+        return carry
+
+    lax.fori_loop(0, ITERS * groups, drain, 0)
     for g in range(groups):
-        store(out, buf, out_sem, ITERS % 2, base(g), per, rows, g).wait()
-
-
-def store(out, buf, out_sem, slot, base, per, rows, g):
+        store(out, bufs[ITERS % 2], out_sem, base(g), per, rows, g).wait()
+
+
+def store(out, buf, out_sem, base, per, rows, g):
     return pltpu.make_async_copy(
-        buf.at[slot, :, pl.ds(base, per), pl.ds(PAD, rows), :],
+        buf.at[:, pl.ds(base, per), pl.ds(PAD, rows), :],
         out.at[:, pl.ds(base, per)],
         out_sem.at[g],
     )
@@ -360,7 +377,8 @@
             in_specs=[pl.BlockSpec(memory_space=pl.ANY)] * 4,
             out_specs=pl.BlockSpec(memory_space=pl.ANY),
             scratch_shapes=[
-                pltpu.VMEM((2, 4, levels, rows + 2 * PAD, cols), f32),
+                pltpu.VMEM((4, levels, rows + 2 * PAD, cols), f32),
+                pltpu.VMEM((4, levels, rows + 2 * PAD, cols), f32),
                 pltpu.VMEM((levels, rows, cols), f32),
                 pltpu.VMEM((levels, rows, cols), jnp.int32),
                 pltpu.VMEM((rows, cols), jnp.int32),
@@ -384,7 +402,7 @@
                 dma((ITERS, groups, 4)),
             ],
             compiler_params=pltpu.CompilerParams(
-                collective_id=0, has_side_effects=True, vmem_limit_bytes=40 << 20
+                collective_id=0, has_side_effects=True, vmem_limit_bytes=60 << 20
             ),
             name="adjoint_steps",
         )(adjoint_state, coefficients, mask, bottom)

time: 44.1 us -> 38.1 us (0.86)
  Pallas kernels: 37.9 us -> 34.4 us
  local copies, waits for them, and re-layouts: 5.92 us -> 3.56 us
    pallas_call x1, Pallas kernels: 37.9 us -> 34.4 us  [local(): pl.pallas_call(functools.partial(kernel, n_lon, n_lat, levels, rows, cols...]
    unnamed x9 -> x1, local copies, waits for them, and re-layouts: 5.92 us -> 3.56 us
where the time goes in v1:
time: 38.1 us; the launch traced here: 38 us
  Pallas kernels  34.4 us (90%)
  local copies, waits for them, and re-layouts  3.56 us (9%)
    pallas_call x1, Pallas kernels, local(): pl.pallas_call(functools.partial(kernel, n_lon, n_lat, levels, rows, cols...  34.4 us
    unnamed x1, local copies, waits for them, and re-layouts  3.56 us

profile of v1, /device:TPU:7, one launch (start us, length us, event | category | flops | bytes accessed | tf_op | source)
XLA Modules:
  0.0 38.0 jit_solution(1576103258580413050)
XLA Ops:
  0.0 34.4 %adjoint_steps.1 = f32[4,20,64,128]{3,2,1,0:T(8,128)} custom-call(f32[4,20,64,128]{3,2,1,0:T(8,128)} %state.1, f32[2,64,128]{2,1,0:T(8,128)} %coef.1, s32[20,64,128]{2,1,0:T(8,128)} %mask.1, s32[64,128]{1,0:T(8,128)} %bottom.1), custom_call_target="tpu_custom_call" | custom-call | tf_op jit(solution)/shard_map/adjoint_steps/pallas_call | solution.py:374
  34.4 3.6 %copy.6 = f32[4,20,64,128]{3,2,1,0:T(8,128)} copy(f32[4,20,64,128]{3,2,1,0:T(8,128)} %adjoint_steps.1) | data formatting | bytes 5242880
